TPU v7x, 256 devices: a whole 4x4x8 slice. The times are simulated.
256 devices in a mesh: slab: 32 (over z, y), snap: 8 (over x, core).
Axes of the slice: x: 4, y: 4, z: 8, core: 2. Of those that a mesh axis runs over, the one named last changes fastest.
Arguments:
- flow: bfloat16 [128, 3, 64, 64, 128], P('snap', None, 'slab'), may hold values from -127 to 127
- large_scale: bfloat16 [3, 64, 64, 128], P(None, 'slab'), may hold values from -6 to 6
- modulation: float32 [128, 64], replicated, may hold values from -15 to 15
- metric: float32 [4, 64, 64, 128], P(None, 'slab'), may hold values from -0.5 to 9.6
Outputs:
- whitened: float32 [128, 3, 64, 64, 128], P(None, None, 'slab', 'snap')
All inputs are finite; a program needn't handle non-finite values.
Results may differ from a plain program's by a relative error of at most 0.0003.
Values may be sent and summed in bfloat16 or wider, within the bound.
A program may use at most 64 MiB of HBM per device.

v0:
```python
import jax
import jax.numpy as jnp
from jax import lax
from jax.sharding import PartitionSpec as P

NSITER = 6


def with_halo(block, sides, width):
    for axis, dim in sides:
        count = lax.axis_size(axis)
        forward = [(i, i + 1) for i in range(count - 1)]
        backward = [(target, source) for source, target in forward]
        low = lax.ppermute(
            lax.slice_in_dim(block, block.shape[dim] - width, None, axis=dim), axis, forward
        )
        high = lax.ppermute(lax.slice_in_dim(block, 0, width, axis=dim), axis, backward)
        block = jnp.concatenate([low, block, high], axis=dim)
    return block


def vorticity(velocity, metric):
    metric_x = metric[0]
    shear_xy = metric[1]
    metric_y = metric[2]
    metric_z = metric[3]

    def along_x(values):
        return 0.5 * (values[..., 1:-1, 2:, :] - values[..., 1:-1, :-2, :])

    def along_y(values):
        return 0.5 * (values[..., 2:, 1:-1, :] - values[..., :-2, 1:-1, :])

    def along_z(values):
        center = values[..., 1:-1, 1:-1, :]
        return 0.5 * (jnp.roll(center, -1, -1) - jnp.roll(center, 1, -1))

    def slope_x(values):
        return metric_x * along_x(values) + shear_xy * along_y(values)

    def slope_y(values):
        return metric_y * along_y(values)

    def slope_z(values):
        return metric_z * along_z(values)

    stream = velocity[..., 0, :, :, :]
    normal = velocity[..., 1, :, :, :]
    spanwise = velocity[..., 2, :, :, :]
    around_x = slope_y(spanwise) - slope_z(normal)
    around_y = slope_z(stream) - slope_x(spanwise)
    around_z = slope_x(normal) - slope_y(stream)
    return jnp.stack([around_x, around_y, around_z], axis=-4)


def wrap_columns(values):
    return jnp.concatenate([values[..., -1:, :], values, values[..., :1, :]], axis=-2)


def whitening(correlation):
    identity = jnp.eye(correlation.shape[0], dtype=correlation.dtype)
    frob_scale = jnp.sqrt(jnp.sum(correlation * correlation) + 1e-06)
    approx = correlation / frob_scale
    inverse = identity
    for repeat in range(NSITER):
        factor = 0.5 * (3.0 * identity - jnp.dot(inverse, approx, precision=lax.Precision.HIGHEST))
        approx = jnp.dot(approx, factor, precision=lax.Precision.HIGHEST)
        inverse = jnp.dot(factor, inverse, precision=lax.Precision.HIGHEST)
    return inverse / jnp.sqrt(frob_scale)


def inner_rows(left_rows, right_rows):
    return lax.dot_general(
        left_rows,
        right_rows,
        (((1,), (1,)), ((), ())),
        precision=lax.Precision.HIGHEST,
        preferred_element_type=jnp.float32,
    )


def planes_padded(flow, large_scale):
    joined = jnp.concatenate([flow, large_scale[None]], axis=0)
    return with_halo(joined, (("slab", 2),), 1)


def per_device(flow, large_scale, modulation, metric):
    snap_count = lax.axis_size("snap")
    slab_count = lax.axis_size("slab")
    own_snaps = flow.shape[0]
    block_cols = flow.shape[3] // snap_count
    snap_index = lax.axis_index("snap")
    mod_ext = jnp.concatenate([modulation[:, -1:], modulation, modulation[:, :1]], axis=1)
    padded = planes_padded(flow, large_scale)
    large_ext = wrap_columns(padded[own_snaps].astype(jnp.float32))
    mod_mine = lax.dynamic_slice_in_dim(mod_ext, snap_index * own_snaps, own_snaps, 0)
    velocity = (
        wrap_columns(padded[:own_snaps].astype(jnp.float32))
        + mod_mine[:, None, None, :, None] * large_ext[None]
    )
    local_fields = vorticity(velocity, metric)
    pieces = local_fields.reshape(
        own_snaps, 3, local_fields.shape[2], snap_count, block_cols, local_fields.shape[4]
    )
    fields = lax.all_to_all(pieces, "snap", split_axis=3, concat_axis=0, tiled=True)[:, :, :, 0]
    snapshot_rows = fields.reshape(fields.shape[0], -1)
    gram_local = inner_rows(snapshot_rows, snapshot_rows)
    gram_total = lax.psum(gram_local, ("slab", "snap"))
    correlation = gram_total / (snapshot_rows.shape[1] * slab_count * snap_count)
    weights = whitening(correlation)
    result = jnp.dot(weights, snapshot_rows, precision=lax.Precision.HIGHEST)
    return result.reshape(fields.shape)


def solution(mesh):
    return jax.shard_map(
        per_device,
        mesh=mesh,
        in_specs=(
            P("snap", None, "slab", None, None),
            P(None, "slab", None, None),
            P(),
            P(None, "slab", None, None),
        ),
        out_specs=P(None, None, "slab", "snap", None),
        check_vma=False,
    )
```

profile of v0, /device:TPU:1, one launch (start us, length us, event | category | flops | bytes accessed | tf_op | source)
XLA Modules:
  0.0 358.1 jit_solution(2387422955889473556)
XLA Ops:
  6.5 2.9 fusion.21
  9.4 4.1 %collective-permute-start = (bf16[17,3,1,64,128]{4,3,2,1,0:T(8,128)(2,1)}, bf16[17,3,1,64,128]{4,3,2,1,0:T(8,128)(2,1)S(1)}, u32[]{:S(2)}, u32[]{:S(2)}) collective-permute-start(bf16[17,3,1,64,128]{4,3,2,1,0:T(8,128)(2,1)} %get-tuple-element.20), channel_id=1, source_target_pairs={{0,8},{8,16},{16,24},{24,32},{32,40},{40,48},{48,56},{56,64},{64,7... | collective-permute-start | bytes 2506760 | tf_op jit(solution)/shard_map/ppermute | solution.py:14
  13.5 1.3 collective-permute-start.1
  15.0 1.0 multiply_bitcast_fusion.2
  15.9 15.1 %collective-permute-done = bf16[17,3,1,64,128]{4,3,2,1,0:T(8,128)(2,1)S(1)} collective-permute-done((bf16[17,3,1,64,128]{4,3,2,1,0:T(8,128)(2,1)}, bf16[17,3,1,64,128]{4,3,2,1,0:T(8,128)(2,1)S(1)}, u32[]{:S(2)}, u32[]{:S(2)}) %collective-permute-start) | collective-permute-done | bytes 835616 | tf_op jit(solution)/shard_map/ppermute | solution.py:14
  31.0 3.8 %collective-permute-done.1 = bf16[17,3,1,64,128]{4,3,2,1,0:T(8,128)(2,1)S(1)} collective-permute-done((bf16[17,3,1,64,128]{4,3,2,1,0:T(8,128)(2,1)}, bf16[17,3,1,64,128]{4,3,2,1,0:T(8,128)(2,1)S(1)}, u32[]{:S(2)}, u32[]{:S(2)}) %collective-permute-start.1) | collective-permute-done | bytes 835616 | tf_op jit(solution)/shard_map/ppermute | solution.py:17
  34.8 0.5 pad_maximum_fusion
  35.3 0.7 slice_convert_fusion
  36.3 1.5 maximum_add_fusion
  37.7 0.5 slice_bitcast_fusion.2
  38.2 0.9 fusion.28
  39.1 0.9 fusion.29
  40.0 0.8 fusion.9
  40.7 1.5 fusion.19
  42.8 43.4 %all_to_all.15 = f32[16,3,2,8,8,128]{5,4,2,1,0,3:T(8,128)} all-to-all(f32[16,3,2,8,8,128]{5,4,2,1,0,3:T(8,128)S(1)} %copy.19), channel_id=1, replica_groups=mesh['slab'=32,'snap'=8] {'snap'}, dimensions={3} | all-to-all | bytes 6291456 | tf_op jit(solution)/shard_map/all_to_all | solution.py:105
  86.2 2.8 reshape_squeeze.3
  89.0 3.2 fusion.34
  92.2 2.4 copy.16
  94.6 242.7 %all-reduce.2.cloned.1.call-done = f32[128,128]{1,0:T(8,128)} async-done(((f32[128,128]{1,0:T(8,128)}), f32[128,128]{1,0:T(8,128)}) %all-reduce.2.cloned.1.call-update) | async-done | bytes 65552 | tf_op jit(solution)/shard_map/psum | solution.py:108
  337.3 1.5 multiply_reduce_fusion
  339.5 1.0 fusion.6
  340.7 1.0 fusion.24
  344.7 3.0 fusion.43
  347.8 3.5 copy.17
  (34 shorter events, 4.0 us)
Async XLA Ops:
  6.5 28.2 %copy-start = (bf16[16,3,2,64,128]{4,3,2,1,0:T(8,128)(2,1)S(1)}, bf16[16,3,2,64,128]{4,3,2,1,0:T(8,128)(2,1)}, u32[]{:S(2)}) copy-start(bf16[16,3,2,64,128]{4,3,2,1,0:T(8,128)(2,1)} %param.4) | copy-start | bytes 4718596
  6.5 28.2 %copy-start.2 = (bf16[3,2,64,128]{3,2,1,0:T(8,128)(2,1)S(1)}, bf16[3,2,64,128]{3,2,1,0:T(8,128)(2,1)}, u32[]{:S(2)}) copy-start(bf16[3,2,64,128]{3,2,1,0:T(8,128)(2,1)} %param.5) | copy-start | bytes 294916
  6.5 8.2 %copy-start.3 = (f32[128,64]{0,1:T(8,128)S(1)}, f32[128,64]{0,1:T(8,128)}, u32[]{:S(2)}) copy-start(f32[128,64]{0,1:T(8,128)} %param.6) | copy-start | bytes 98308
  6.5 330.8 %all-reduce.2.cloned.1.call-start = ((), (), s32[]{:S(2)}) async-start(), calls=%async_computation.1 | async-start | bytes 131072 | tf_op jit(solution)/shard_map/psum | solution.py:108
  9.4 21.6 %collective-permute-start = (bf16[17,3,1,64,128]{4,3,2,1,0:T(8,128)(2,1)}, bf16[17,3,1,64,128]{4,3,2,1,0:T(8,128)(2,1)S(1)}, u32[]{:S(2)}, u32[]{:S(2)}) collective-permute-start(bf16[17,3,1,64,128]{4,3,2,1,0:T(8,128)(2,1)} %get-tuple-element.20), channel_id=1, source_target_pairs={{0,8},{8,16},{16,24},{24,32},{32,40},{40,48},{48,56},{56,64},{64,7... | collective-permute-start | bytes 2506760 | tf_op jit(solution)/shard_map/ppermute | solution.py:14
  13.5 21.3 %collective-permute-start.1 = (bf16[17,3,1,64,128]{4,3,2,1,0:T(8,128)(2,1)}, bf16[17,3,1,64,128]{4,3,2,1,0:T(8,128)(2,1)S(1)}, u32[]{:S(2)}, u32[]{:S(2)}) collective-permute-start(bf16[17,3,1,64,128]{4,3,2,1,0:T(8,128)(2,1)} %get-tuple-element.21), channel_id=1, source_target_pairs={{8,0},{16,8},{24,16},{32,24},{40,32},{48,40},{56,48},{64,56},{72,6... | collective-permute-start | bytes 2506760 | tf_op jit(solution)/shard_map/ppermute | solution.py:17
  94.6 250.2 %copy-start.1 = (f32[6144,128]{1,0:T(8,128)S(1)}, f32[6144,128]{1,0:T(8,128)}, u32[]{:S(2)}) copy-start(f32[6144,128]{1,0:T(8,128)} %copy.16) | copy-start | bytes 9437188
Sparse Core Ops, SparseCore 0:
  92.3 244.9 all-reduce.1
where the time goes:
time: 358 us
  waiting for transfers between devices  262 us (73%)
  blocking collectives  43.4 us (12%)
  between operations  14.4 us (4%)
  local copies, waits for them, and re-layouts  11.3 us (3%)
  matrix products  11.3 us (3%)
  other arithmetic  10.6 us (3%)
  starting transfers between devices  5.35 us (1%)
    psum x1, waiting for transfers between devices, per_device(): gram_total = lax.psum(gram_local, ('slab', 'snap'))  243 us
    all_to_all x1, blocking collectives, per_device(): lax.all_to_all(pieces, 'snap', split_axis=3, concat_axis=0, tiled=True)  43.4 us
    ppermute x1, waiting for transfers between devices, with_halo(): lax.ppermute(lax.slice_in_dim(block, block.shape[dim] - width, None, axis...  15.1 us
  transfers between devices with their start and end apart: 3, of which 3 were waited for; matrix products, arithmetic and copies ran while one was open for 1% of the time, Pallas kernels for 0%

commit v1 on v0

--- a/solution.py
+++ b/solution.py
@@ -105,7 +105,9 @@
     fields = lax.all_to_all(pieces, "snap", split_axis=3, concat_axis=0, tiled=True)[:, :, :, 0]
     snapshot_rows = fields.reshape(fields.shape[0], -1)
     gram_local = inner_rows(snapshot_rows, snapshot_rows)
-    gram_total = lax.psum(gram_local, ("slab", "snap"))
+    gram_total = gram_local
+    for kk in ("snap", "slab"):
+        gram_total = lax.psum(gram_total, kk)
     correlation = gram_total / (snapshot_rows.shape[1] * slab_count * snap_count)
     weights = whitening(correlation)
     result = jnp.dot(weights, snapshot_rows, precision=lax.Precision.HIGHEST)

time: 358 us -> 325 us (0.908); the launches traced: 358 us -> 321 us
  waiting for transfers between devices: 262 us -> 224 us
    psum x1 -> x2, waiting for transfers between devices: 243 us -> 205 us  [per_device(): gram_total = lax.psum(gram_total, kk)]
  transfers between devices with their start and end apart: 3 -> 4, of which waited for: 3 -> 4; matrix products, arithmetic and copies ran while one was open for 1% -> 1% of each run, Pallas kernels for 0% -> 0%
where the time goes in v1:
time: 325 us; the launch traced here: 321 us
  waiting for transfers between devices  224 us (69%)
  blocking collectives  43.4 us (13%)
  between operations  14.4 us (4%)
  local copies, waits for them, and re-layouts  11.3 us (3%)
  matrix products  11.3 us (3%)
  other arithmetic  10.6 us (3%)
  starting transfers between devices  5.58 us (2%)
    psum x2, waiting for transfers between devices, per_device(): gram_total = lax.psum(gram_total, kk)  205 us
    all_to_all x1, blocking collectives, per_device(): lax.all_to_all(pieces, 'snap', split_axis=3, concat_axis=0, tiled=True)  43.4 us
    ppermute x1, waiting for transfers between devices, with_halo(): lax.ppermute(lax.slice_in_dim(block, block.shape[dim] - width, None, axis...  15.1 us
  transfers between devices with their start and end apart: 4, of which 4 were waited for; matrix products, arithmetic and copies ran while one was open for 1% of the time, Pallas kernels for 0%

profile of v1, /device:TPU:1, one launch (start us, length us, event | category | flops | bytes accessed | tf_op | source)
XLA Modules:
  0.0 320.7 jit_solution(1808722653167383652)
XLA Ops:
  6.5 2.9 fusion.21
  9.4 4.1 %collective-permute-start = (bf16[17,3,1,64,128]{4,3,2,1,0:T(8,128)(2,1)}, bf16[17,3,1,64,128]{4,3,2,1,0:T(8,128)(2,1)S(1)}, u32[]{:S(2)}, u32[]{:S(2)}) collective-permute-start(bf16[17,3,1,64,128]{4,3,2,1,0:T(8,128)(2,1)} %get-tuple-element.20), channel_id=1, source_target_pairs={{0,8},{8,16},{16,24},{24,32},{32,40},{40,48},{48,56},{56,64},{64,7... | collective-permute-start | bytes 2506760 | tf_op jit(solution)/shard_map/ppermute | solution.py:14
  13.5 1.3 collective-permute-start.1
  15.0 1.0 multiply_bitcast_fusion.2
  15.9 15.1 %collective-permute-done = bf16[17,3,1,64,128]{4,3,2,1,0:T(8,128)(2,1)S(1)} collective-permute-done((bf16[17,3,1,64,128]{4,3,2,1,0:T(8,128)(2,1)}, bf16[17,3,1,64,128]{4,3,2,1,0:T(8,128)(2,1)S(1)}, u32[]{:S(2)}, u32[]{:S(2)}) %collective-permute-start) | collective-permute-done | bytes 835616 | tf_op jit(solution)/shard_map/ppermute | solution.py:14
  31.0 3.8 %collective-permute-done.1 = bf16[17,3,1,64,128]{4,3,2,1,0:T(8,128)(2,1)S(1)} collective-permute-done((bf16[17,3,1,64,128]{4,3,2,1,0:T(8,128)(2,1)}, bf16[17,3,1,64,128]{4,3,2,1,0:T(8,128)(2,1)S(1)}, u32[]{:S(2)}, u32[]{:S(2)}) %collective-permute-start.1) | collective-permute-done | bytes 835616 | tf_op jit(solution)/shard_map/ppermute | solution.py:17
  34.8 0.5 pad_maximum_fusion
  35.3 0.7 slice_convert_fusion
  36.3 1.5 maximum_add_fusion
  38.2 0.9 fusion.28
  39.1 0.9 fusion.29
  40.0 0.8 fusion.9
  40.7 1.5 fusion.19
  42.8 43.4 %all_to_all.15 = f32[16,3,2,8,8,128]{5,4,2,1,0,3:T(8,128)} all-to-all(f32[16,3,2,8,8,128]{5,4,2,1,0,3:T(8,128)S(1)} %copy.19), channel_id=1, replica_groups=mesh['slab'=32,'snap'=8] {'snap'}, dimensions={3} | all-to-all | bytes 6291456 | tf_op jit(solution)/shard_map/all_to_all | solution.py:105
  86.2 2.8 reshape_squeeze.3
  89.0 3.2 %fusion.34 = f32[128,128]{1,0:T(8,128)} fusion(f32[128,6144]{1,0:T(8,128)S(1)} %reshape_squeeze.3), kind=kOutput, calls=%fused_computation.69 | convolution fusion | flops 1207959552 | bytes 3211264 | tf_op jit(solution)/shard_map/dot_general | solution.py:73
  92.4 65.9 %all-reduce.3.cloned.1.call-done = f32[128,128]{1,0:T(8,128)} async-done(((f32[128,128]{1,0:T(8,128)}), f32[128,128]{1,0:T(8,128)}) %all-reduce.3.cloned.1.call-update) | async-done | bytes 65552 | tf_op jit(solution)/shard_map/psum | solution.py:110
  158.4 2.4 copy.16
  160.7 139.2 %all-reduce.5.cloned.1.call-done = f32[128,128]{1,0:T(8,128)} async-done(((f32[128,128]{1,0:T(8,128)}), f32[128,128]{1,0:T(8,128)}) %all-reduce.5.cloned.1.call-update) | async-done | bytes 65552 | tf_op jit(solution)/shard_map/psum | solution.py:110
  299.9 1.5 multiply_reduce_fusion
  302.1 1.0 fusion.6
  303.3 1.0 fusion.24
  307.4 3.0 fusion.43
  310.4 3.5 %copy.17 = f32[128,3,2,8,128]{4,3,2,1,0:T(8,128)} copy(f32[128,3,2,8,128]{4,0,3,2,1:T(8,128)S(1)} %fusion.43) | data formatting | bytes 6291456 | tf_op jit(solution)/shard_map/dot_general | solution.py:113
  (37 shorter events, 4.7 us)
Async XLA Ops:
  6.5 28.2 %copy-start = (bf16[16,3,2,64,128]{4,3,2,1,0:T(8,128)(2,1)S(1)}, bf16[16,3,2,64,128]{4,3,2,1,0:T(8,128)(2,1)}, u32[]{:S(2)}) copy-start(bf16[16,3,2,64,128]{4,3,2,1,0:T(8,128)(2,1)} %param.4) | copy-start | bytes 4718596
  6.5 28.2 %copy-start.2 = (bf16[3,2,64,128]{3,2,1,0:T(8,128)(2,1)S(1)}, bf16[3,2,64,128]{3,2,1,0:T(8,128)(2,1)}, u32[]{:S(2)}) copy-start(bf16[3,2,64,128]{3,2,1,0:T(8,128)(2,1)} %param.5) | copy-start | bytes 294916
  6.5 8.2 %copy-start.3 = (f32[128,64]{0,1:T(8,128)S(1)}, f32[128,64]{0,1:T(8,128)}, u32[]{:S(2)}) copy-start(f32[128,64]{0,1:T(8,128)} %param.6) | copy-start | bytes 98308
  6.5 151.8 %all-reduce.3.cloned.1.call-start = ((), (), s32[]{:S(2)}) async-start(), calls=%async_computation.1 | async-start | bytes 131072 | tf_op jit(solution)/shard_map/psum | solution.py:110
  9.4 21.6 %collective-permute-start = (bf16[17,3,1,64,128]{4,3,2,1,0:T(8,128)(2,1)}, bf16[17,3,1,64,128]{4,3,2,1,0:T(8,128)(2,1)S(1)}, u32[]{:S(2)}, u32[]{:S(2)}) collective-permute-start(bf16[17,3,1,64,128]{4,3,2,1,0:T(8,128)(2,1)} %get-tuple-element.20), channel_id=1, source_target_pairs={{0,8},{8,16},{16,24},{24,32},{32,40},{40,48},{48,56},{56,64},{64,7... | collective-permute-start | bytes 2506760 | tf_op jit(solution)/shard_map/ppermute | solution.py:14
  13.5 21.3 %collective-permute-start.1 = (bf16[17,3,1,64,128]{4,3,2,1,0:T(8,128)(2,1)}, bf16[17,3,1,64,128]{4,3,2,1,0:T(8,128)(2,1)S(1)}, u32[]{:S(2)}, u32[]{:S(2)}) collective-permute-start(bf16[17,3,1,64,128]{4,3,2,1,0:T(8,128)(2,1)} %get-tuple-element.21), channel_id=1, source_target_pairs={{8,0},{16,8},{24,16},{32,24},{40,32},{48,40},{56,48},{64,56},{72,6... | collective-permute-start | bytes 2506760 | tf_op jit(solution)/shard_map/ppermute | solution.py:17
  92.2 207.7 %all-reduce.5.cloned.1.call-start = ((), (), s32[]{:S(2)}) async-start(), calls=%async_computation.2 | async-start | bytes 131072 | tf_op jit(solution)/shard_map/psum | solution.py:110
  160.7 146.6 %copy-start.1 = (f32[6144,128]{1,0:T(8,128)S(1)}, f32[6144,128]{1,0:T(8,128)}, u32[]{:S(2)}) copy-start(f32[6144,128]{1,0:T(8,128)} %copy.16) | copy-start | bytes 9437188
Sparse Core Ops, SparseCore 0:
  92.3 65.9 all-reduce.2
  161.8 138.0 all-reduce.4
